TPU v7x, 32 devices: a whole 2x2x4 slice. The times are simulated.
32 devices in a mesh: seq: 8 (over z, x), head: 4 (over y, core).
Axes of the slice: x: 2, y: 2, z: 4, core: 2. Of those that a mesh axis runs over, the one named last changes fastest.
Arguments:
- hidden_states: bfloat16 [2, 352, 5120], P(None, 'seq', 'head'), may hold values from -60 to 60
- clean_states: bfloat16 [2, 352, 5120], P(None, 'seq', 'head'), may hold values from -60 to 60
- w_query: bfloat16 [5120, 2560], P(None, 'head'), may hold values from -2 to 2
- w_key: bfloat16 [5120, 2560], P(None, 'head'), may hold values from -2 to 2
- w_value: bfloat16 [5120, 2560], P(None, 'head'), may hold values from -0.078125 to 0.078125
- q_gain: float32 [2560], P('head'), may hold values from 0.1 to 1.9
- k_gain: float32 [2560], P('head'), may hold values from 0.1 to 1.9
- cache_keys: bfloat16 [9, 352, 2560], P(None, 'seq', 'head'), may hold values from -1300 to 1300
- cache_values: bfloat16 [9, 352, 2560], P(None, 'seq', 'head'), may hold values from -6 to 6
- modulation: float32 [4, 2, 5120], replicated, may hold values from -3 to 3
- controls: int32 [3], replicated, may hold values from 0 to 6, as said below
- frame_pos: int32 [11], replicated, may hold values from 0 to 63
Outputs:
- attention_out: bfloat16 [2, 352, 2560], P(None, 'seq', 'head')
- new_keys: bfloat16 [9, 352, 2560], P(None, 'seq', 'head')
- new_values: bfloat16 [9, 352, 2560], P(None, 'seq', 'head')
Inputs may be any that keep to these rules, and one draw needn't show every extreme that they name: controls[0] lies in 1 to 3, controls[1] in 0 to 6 and equal to 6 whenever controls[0] is below 3, controls[2] in 1 to 2.
All inputs are finite; a program needn't handle non-finite values.
Results may differ from a plain program's by a relative error of at most 0.011.
The roundings to bfloat16 on the way count: a program that leaves them out, or rounds other values in their place, can miss the bound.
Values may be sent and summed in bfloat16 or wider, within the bound.
A program may use at most 320 MiB of HBM per device.

v0:
```python
import jax
import jax.numpy as jnp
from jax import lax
from jax.sharding import PartitionSpec as P

HD = 128
epsilon = 1e-06


def modulate(states, modulation, step_index):
    choose = (jnp.arange(modulation.shape[0], dtype=jnp.int32) == step_index).astype(jnp.float32)
    picked = jnp.sum(choose[:, None, None] * modulation, axis=0)
    values = states.astype(jnp.float32)
    centre = jnp.mean(values, axis=-1, keepdims=True)
    spread = jnp.mean(jnp.square(values - centre), axis=-1, keepdims=True)
    normed = (values - centre) * lax.rsqrt(spread + epsilon)
    return (normed * (1.0 + picked[1]) + picked[0]).astype(jnp.bfloat16)


def rms_scale(values, square_total, width, gain):
    return values * lax.rsqrt(square_total / width + epsilon)[:, None] * gain


def rotate(values, time_pos, space_pos):
    head_size = values.shape[-1]
    half_size = head_size // 2
    time_pairs = (head_size - 4 * (head_size // 6)) // 2
    space_pairs = half_size - time_pairs
    pair_index = jnp.arange(half_size, dtype=jnp.int32)
    exponent = jnp.where(
        pair_index < time_pairs, pair_index / time_pairs, (pair_index - time_pairs) / space_pairs
    ).astype(jnp.float32)
    frequency = jnp.power(10000.0, -exponent)
    is_time = (pair_index < time_pairs)[None, None, :]
    position = jnp.where(
        is_time,
        time_pos.astype(jnp.float32)[:, None, None],
        space_pos.astype(jnp.float32)[None, :, None],
    )
    angle = position * frequency
    cosine = jnp.cos(angle)[:, :, None, :]
    sine = jnp.sin(angle)[:, :, None, :]
    first = values[..., :half_size]
    second = values[..., half_size:]
    return jnp.concatenate(
        [first * cosine - second * sine, second * cosine + first * sine], axis=-1
    )


def write_cache(key_store, value_store, fresh_keys, fresh_values, slot_start, sinks):
    rolling = key_store.shape[0] - sinks
    for group_frame in range(fresh_keys.shape[0]):
        target = sinks + (slot_start + group_frame) % rolling
        anchor = (target, jnp.int32(0), jnp.int32(0))
        key_store = lax.dynamic_update_slice(
            key_store, fresh_keys[group_frame : group_frame + 1], anchor
        )
        value_store = lax.dynamic_update_slice(
            value_store, fresh_values[group_frame : group_frame + 1], anchor
        )
    return (key_store, value_store)


def body(
    hidden_states,
    clean_states,
    w_query,
    w_key,
    w_value,
    q_gain,
    k_gain,
    cache_keys,
    cache_values,
    modulation,
    controls,
    frame_pos,
):
    timestep = controls[0]
    write_slot = controls[1]
    sink_count = controls[2]
    full_hidden, full_clean = (
        lax.all_gather(hidden_states, "head", axis=2, tiled=True),
        lax.all_gather(clean_states, "head", axis=2, tiled=True),
    )
    group_count, local_frame, model_width = full_hidden.shape
    local_rows = group_count * local_frame
    cache_count = cache_keys.shape[0]
    local_inner = w_query.shape[1]
    head_size = HD
    local_heads = local_inner // head_size
    inner_width = local_inner * lax.axis_size("head")
    noisy = modulate(full_hidden, modulation, timestep).reshape(local_rows, model_width)
    settled = modulate(full_clean, modulation, jnp.int32(0)).reshape(local_rows, model_width)
    query_raw = jnp.dot(noisy, w_query, preferred_element_type=jnp.float32)
    key_raw = jnp.dot(noisy, w_key, preferred_element_type=jnp.float32)
    key_clean = jnp.dot(settled, w_key, preferred_element_type=jnp.float32)
    value_new = jnp.dot(noisy, w_value, preferred_element_type=jnp.float32).astype(jnp.bfloat16)
    value_clean = jnp.dot(settled, w_value, preferred_element_type=jnp.float32).astype(jnp.bfloat16)
    square_query, square_key, square_clean = lax.psum(
        (
            jnp.sum(query_raw * query_raw, axis=-1),
            jnp.sum(key_raw * key_raw, axis=-1),
            jnp.sum(key_clean * key_clean, axis=-1),
        ),
        "head",
    )
    query_norm = rms_scale(query_raw, square_query, inner_width, q_gain)
    key_norm = rms_scale(key_raw, square_key, inner_width, k_gain)
    stored_keys = rms_scale(key_clean, square_clean, inner_width, k_gain).astype(jnp.bfloat16)
    space_pos = lax.axis_index("seq") * local_frame + jnp.arange(local_frame, dtype=jnp.int32)
    group_time = frame_pos[cache_count:]
    cache_time = frame_pos[:cache_count]
    query_rot = (
        rotate(
            query_norm.reshape(group_count, local_frame, local_heads, head_size),
            group_time,
            space_pos,
        )
        .astype(jnp.bfloat16)
        .reshape(group_count, local_frame, local_inner)
    )
    key_rot = (
        rotate(
            key_norm.reshape(group_count, local_frame, local_heads, head_size),
            group_time,
            space_pos,
        )
        .astype(jnp.bfloat16)
        .reshape(group_count, local_frame, local_inner)
    )
    cache_rot = (
        rotate(
            cache_keys.astype(jnp.float32).reshape(
                cache_count, local_frame, local_heads, head_size
            ),
            cache_time,
            space_pos,
        )
        .astype(jnp.bfloat16)
        .reshape(cache_count, local_frame, local_inner)
    )
    key_local = jnp.concatenate([cache_rot, key_rot], axis=0)
    value_local = jnp.concatenate(
        [cache_values, value_new.reshape(group_count, local_frame, local_inner)], axis=0
    )
    scale = head_size ** (-0.5)
    query_whole = lax.all_gather(query_rot, "seq", axis=1, tiled=True)
    all_rows = query_whole.shape[0] * query_whole.shape[1]
    scores = (
        jnp.einsum(
            "qhd,khd->hqk",
            query_whole.reshape(all_rows, local_heads, head_size),
            key_local.reshape(-1, local_heads, head_size),
            preferred_element_type=jnp.float32,
        )
        * scale
    )
    top_score = lax.pmax(jnp.max(scores, axis=-1), "seq")
    weights = jnp.exp(scores - top_score[..., None])
    totals = jnp.sum(weights, axis=-1)
    summed = jnp.einsum(
        "hqk,khd->qhd",
        weights.astype(jnp.bfloat16),
        value_local.reshape(-1, local_heads, head_size),
        preferred_element_type=jnp.float32,
    )
    summed_part, totals_part = (
        lax.psum_scatter(
            summed.reshape(group_count, -1, local_inner), "seq", scatter_dimension=1, tiled=True
        ),
        lax.psum_scatter(
            jnp.transpose(totals).reshape(group_count, -1, local_heads),
            "seq",
            scatter_dimension=1,
            tiled=True,
        ),
    )
    attended = (
        summed_part.reshape(local_rows, local_heads, head_size)
        / totals_part.reshape(local_rows, local_heads)[:, :, None]
    )
    attention_out = attended.reshape(group_count, local_frame, local_inner).astype(jnp.bfloat16)
    new_keys, new_values = write_cache(
        cache_keys,
        cache_values,
        stored_keys.reshape(group_count, local_frame, local_inner),
        value_clean.reshape(group_count, local_frame, local_inner),
        write_slot,
        sink_count,
    )
    return (attention_out, new_keys, new_values)


def solution(mesh):
    in_specs = (
        P(None, "seq", "head"),
        P(None, "seq", "head"),
        P(None, "head"),
        P(None, "head"),
        P(None, "head"),
        P("head"),
        P("head"),
        P(None, "seq", "head"),
        P(None, "seq", "head"),
        P(),
        P(),
        P(),
    )
    out_specs = (P(None, "seq", "head"), P(None, "seq", "head"), P(None, "seq", "head"))
    return jax.shard_map(body, mesh=mesh, in_specs=in_specs, out_specs=out_specs, check_vma=False)
```

profile of v0, /device:TPU:0, one launch (start us, length us, event | category | flops | bytes accessed | tf_op | source)
XLA Modules:
  0.0 270.5 jit_solution(3133796648397645756)
XLA Ops:
  7.2 1.9 copy.76
  9.2 1.1 copy.77
  11.9 1.6 fusion.26
  13.5 10.7 %all_gather.9 = bf16[2,44,5120]{2,0,1:T(2,128)(2,1)S(1)} all-gather(bf16[2,44,1280]{2,0,1:T(2,128)(2,1)S(1)} %copy-done.4), channel_id=1, replica_groups=mesh['seq'=8,'head'=4] {'head'}, dimensions={2}, use_global_device_ids=true | all-gather | bytes 1126400 | tf_op jit(solution)/shard_map/all_gather | solution.py:82
  25.0 1.3 fusion.14
  26.6 1.7 fusion.17
  28.8 4.0 %convolution_convert_fusion.1 = bf16[88,640]{1,0:T(8,128)(2,1)S(1)} fusion(bf16[88,5120]{1,0:T(8,128)(2,1)S(1)} %reshape.149, bf16[5120,640]{1,0:T(8,128)(2,1)} %param.16), kind=kOutput, calls=%fused_computation.27 | convolution fusion | flops 576773120 | bytes 7567360 | tf_op jit(solution)/shard_map/dot_general | solution.py:97
  32.8 4.2 %multiply_reduce_fusion.2 = (f32[88]{0:T(128)S(1)}, f32[88,640]{1,0:T(8,128)S(1)}) fusion(bf16[88,5120]{1,0:T(8,128)(2,1)S(1)} %reshape.149, bf16[5120,640]{1,0:T(8,128)(2,1)} %param.15), kind=kOutput, calls=%fused_computation.43 | convolution fusion | flops 576829376 | bytes 7680352 | tf_op jit(solution)/shard_map/dot_general | solution.py:95
  37.0 4.2 %multiply_reduce_fusion.3 = (f32[88]{0:T(128)S(1)}, f32[88,640]{1,0:T(8,128)S(1)}) fusion(bf16[88,5120]{1,0:T(8,128)(2,1)S(1)} %reshape.149, bf16[5120,640]{1,0:T(8,128)(2,1)} %param.14), kind=kOutput, calls=%fused_computation.45 | convolution fusion | flops 576829376 | bytes 7680352 | tf_op jit(solution)/shard_map/dot_general | solution.py:94
  41.3 1.7 reshape.151
  42.9 9.5 %all_gather.11 = bf16[2,44,5120]{2,0,1:T(2,128)(2,1)S(1)} all-gather(bf16[2,44,1280]{2,0,1:T(2,128)(2,1)S(1)} %copy-done.5), channel_id=1, replica_groups=mesh['seq'=8,'head'=4] {'head'}, dimensions={2}, use_global_device_ids=true | all-gather | bytes 1126400 | tf_op jit(solution)/shard_map/all_gather | solution.py:83
  53.2 1.3 fusion.10
  54.5 1.7 fusion.13
  56.7 4.2 %multiply_reduce_fusion.1 = (f32[88]{0:T(128)S(1)}, f32[88,640]{1,0:T(8,128)S(1)}) fusion(bf16[88,5120]{1,0:T(8,128)(2,1)S(1)} %reshape.160, bf16[5120,640]{1,0:T(8,128)(2,1)} %param.15), kind=kOutput, calls=%fused_computation.41 | convolution fusion | flops 576829376 | bytes 7680352 | tf_op jit(solution)/shard_map/dot_general | solution.py:96
  60.8 6.7 %all-reduce.2 = (f32[88]{0:T(128)S(1)}, f32[88]{0:T(128)S(1)}, f32[88]{0:T(128)S(1)}) all-reduce(f32[88]{0:T(128)S(1)} %get-tuple-element.38, f32[88]{0:T(128)S(1)} %get-tuple-element.40, f32[88]{0:T(128)S(1)} %get-tuple-element.42), channel_id=1, replica_groups=mesh['seq'=8,'head'=4] {'head'}, use_global_device_ids=true, to_apply=%region_4.0 | all-reduce | flops 264 | bytes 2112 | tf_op jit(solution)/shard_map/psum | solution.py:99
  69.0 0.8 reshape.164
  70.2 33.1 %all_gather.10 = bf16[2,352,640]{2,0,1:T(2,128)(2,1)S(1)} all-gather(bf16[2,44,640]{2,0,1:T(2,128)(2,1)S(1)} %copy.56), channel_id=1, replica_groups=mesh['seq'=8,'head'=4] {'seq'}, dimensions={1}, use_global_device_ids=true | all-gather | bytes 1013760 | tf_op jit(solution)/shard_map/all_gather | solution.py:147
  103.3 1.7 copy.43
  105.8 1.6 reshape.162
  107.4 1.7 subtract_convert_fusion
  110.3 1.7 reshape.157
  112.0 5.6 %multiply_reduce_fusion = (f32[5,704]{1,0:T(8,128)S(1)}, f32[5,704,484]{2,1,0:T(8,128)}) fusion(bf16[704,5,128]{0,2,1:T(8,128)(2,1)S(1)} %reshape.153, bf16[484,5,128]{2,1,0:T(8,128)(2,1)} %reshape.157), kind=kOutput, calls=%fused_computation.1 | convolution fusion | flops 439545920 | bytes 8349440 | tf_op jit(solution)/shard_map/qhd,khd->hqk/dot_general | solution.py:150
  117.7 36.5 %pmax.7 = f32[5,704]{1,0:T(8,128)S(1)} all-reduce(f32[5,704]{1,0:T(8,128)S(1)} %get-tuple-element.44), channel_id=1, replica_groups=mesh['seq'=8,'head'=4] {'seq'}, use_global_device_ids=true, to_apply=%region_8.0 | all-reduce | flops 3520 | bytes 28160 | tf_op jit(solution)/shard_map/pmax | solution.py:158
  154.2 5.7 %fusion.18 = f32[704,5,128]{2,0,1:T(8,128)} fusion(f32[5,704,484]{2,1,0:T(8,128)} %get-tuple-element.45, f32[5,704]{1,0:T(8,128)S(1)} %pmax.7, bf16[484,5,128]{2,1,0:T(8,128)(2,1)S(1)} %copy-done), kind=kOutput, calls=%fused_computation.25 | convolution fusion | flops 441253120 | bytes 9250560 | tf_op jit(solution)/shard_map/hqk,khd->qhd/dot_general | solution.py:161
  159.9 1.9 copy.49
  161.8 2.9 %reshape.158 = f32[2,352,640]{1,0,2:T(2,128)} reshape(f32[704,5,128]{0,2,1:T(8,128)S(1)} %copy.49) | data formatting | bytes 3604480 | tf_op jit(solution)/shard_map/reshape | solution.py:169
  164.7 4.7 %copy.50 = f32[2,352,640]{2,0,1:T(2,128)} copy(f32[2,352,640]{1,0,2:T(2,128)} %reshape.158) | data formatting | bytes 3604480 | tf_op jit(solution)/shard_map/reshape | solution.py:169
  172.4 4.8 %fusion = f32[5,704]{1,0:T(8,128)S(1)} fusion(f32[5,704,484]{2,1,0:T(8,128)} %get-tuple-element.45, f32[5,704]{1,0:T(8,128)S(1)} %pmax.7), kind=kLoop, calls=%fused_computation.2 | loop fusion | flops 5107520 | bytes 6842880 | tf_op jit(solution)/shard_map/reduce_sum | solution.py:160
  178.5 33.9 %all-reduce.1 = f32[2,352,5]{1,0,2:T(2,128)S(1)} all-reduce(f32[2,352,5]{1,0,2:T(2,128)S(1)} %reshape.159), channel_id=3, replica_groups=mesh['seq'=8,'head'=4] {'seq'}, use_global_device_ids=true, to_apply=%region_11.0.clone | all-reduce | flops 3520 | bytes 28160
  212.8 4.1 %convolution_convert_fusion = bf16[88,640]{1,0:T(8,128)(2,1)S(1)} fusion(bf16[88,5120]{1,0:T(8,128)(2,1)S(1)} %reshape.160, bf16[5120,640]{1,0:T(8,128)(2,1)} %param.16), kind=kOutput, calls=%fused_computation.26 | convolution fusion | flops 576773120 | bytes 7567360 | tf_op jit(solution)/shard_map/dot_general | solution.py:98
  219.5 42.4 %all-reduce.5.cloned.1.call-done = f32[2,352,640]{2,0,1:T(2,128)} async-done(((f32[2,352,640]{2,0,1:T(2,128)}), f32[2,352,640]{2,0,1:T(2,128)}) %all-reduce.5.cloned.1.call-update) | async-done | bytes 1802256
  261.9 1.0 constant_dynamic-slice_fusion.1
  (78 shorter events, 12.7 us)
Async XLA Ops:
  7.2 6.4 %copy-start.4 = (bf16[2,44,1280]{2,0,1:T(2,128)(2,1)S(1)}, bf16[2,44,1280]{2,0,1:T(2,128)(2,1)}, u32[]{:S(2)}) copy-start(bf16[2,44,1280]{2,0,1:T(2,128)(2,1)} %param.12) | copy-start | bytes 675844
  7.2 3.2 %copy-start.7 = (s32[3]{0:T(128)S(1)}, s32[3]{0:T(128)}, u32[]{:S(2)}) copy-start(s32[3]{0:T(128)} %param.22) | copy-start | bytes 40
  7.2 3.1 %copy-start.10 = (s32[11]{0:T(128)S(1)}, s32[11]{0:T(128)}, u32[]{:S(2)}) copy-start(s32[11]{0:T(128)} %param.23) | copy-start | bytes 136
  7.2 254.7 %all-reduce.5.cloned.1.call-start = ((), (), s32[]{:S(2)}) async-start(), calls=%async_computation | async-start | bytes 3604480
  10.2 30.9 %copy-start.1 = (bf16[9,44,640]{2,1,0:T(8,128)(2,1)}, bf16[9,44,640]{2,1,0:T(8,128)(2,1)S(1)}, u32[]{:S(2)}) copy-start(bf16[9,44,640]{2,1,0:T(8,128)(2,1)S(1)} %copy.77) | copy-start | bytes 1520644
  11.6 14.7 %copy-start.6 = (f32[4,2,5120]{2,1,0:T(2,128)S(1)}, f32[4,2,5120]{2,1,0:T(2,128)}, u32[]{:S(2)}) copy-start(f32[4,2,5120]{2,1,0:T(2,128)} %param.21) | copy-start | bytes 491524
  41.2 1.8 copy-start.5
  56.6 10.9 %copy-start.8 = (f32[640]{0:T(1024)S(1)}, f32[640]{0:T(1024)}, u32[]{:S(2)}) copy-start(f32[640]{0:T(1024)} %param.18) | copy-start | bytes 7684
  56.7 11.7 %copy-start.9 = (f32[640]{0:T(1024)S(1)}, f32[640]{0:T(1024)}, u32[]{:S(2)}) copy-start(f32[640]{0:T(1024)} %param.17) | copy-start | bytes 7684
  109.1 1.2 copy-start.3
  112.0 42.1 %copy-start = (bf16[484,5,128]{2,1,0:T(8,128)(2,1)S(1)}, bf16[484,5,128]{2,1,0:T(8,128)(2,1)}, u32[]{:S(2)}) copy-start(bf16[484,5,128]{2,1,0:T(8,128)(2,1)} %reshape.151) | copy-start | bytes 1858564
  172.4 4.9 %copy-start.11 = (u32[32]{0:T(128)S(1)}, u32[32]{0:T(128)}, u32[]{:S(2)}) copy-start(u32[32]{0:T(128)} %constant.61) | copy-start | bytes 388
  212.8 4.7 %copy-start.2 = (bf16[88,640]{1,0:T(8,128)(2,1)S(1)}, bf16[88,640]{1,0:T(8,128)(2,1)}, u32[]{:S(2)}) copy-start(bf16[88,640]{1,0:T(8,128)(2,1)} %get-tuple-element.29) | copy-start | bytes 337924
Sparse Core Ops, SparseCore 0:
  169.5 92.3 all-reduce.4
where the time goes:
time: 271 us; the launch traced here: 270 us
  blocking collectives  130 us (48%)
  waiting for transfers between devices  42.4 us (16%)
  matrix products  32 us (12%)
  local copies, waits for them, and re-layouts  28.4 us (10%)
  other arithmetic  19.3 us (7%)
  between operations  18.1 us (7%)
    unnamed x2, waiting for transfers between devices  42.4 us
    pmax x1, blocking collectives, body(): top_score = lax.pmax(jnp.max(scores, axis=-1), 'seq')  36.5 us
    unnamed x1, blocking collectives  33.9 us
    all_gather x1, blocking collectives, body(): query_whole = lax.all_gather(query_rot, 'seq', axis=1, tiled=True)  33.1 us
    all_gather x1, blocking collectives, body(): lax.all_gather(hidden_states, 'head', axis=2, tiled=True)  10.7 us
    all_gather x1, blocking collectives, body(): lax.all_gather(clean_states, 'head', axis=2, tiled=True)  9.48 us
    reshape x2, local copies, waits for them, and re-layouts, body(): summed.reshape(group_count, -1, local_inner)  7.56 us
    psum x1, blocking collectives, body(): lax.psum((jnp.sum(query_raw * query_raw, axis=-1), jnp.sum(key_raw * key_...  6.68 us
  transfers between devices with their start and end apart: 1, of which 1 were waited for; matrix products, arithmetic and copies ran while one was open for 5% of the time, Pallas kernels for 0%

commit v1 on v0

--- a/solution.py
+++ b/solution.py
@@ -144,7 +144,14 @@
         [cache_values, value_new.reshape(group_count, local_frame, local_inner)], axis=0
     )
     scale = head_size ** (-0.5)
-    query_whole = lax.all_gather(query_rot, "seq", axis=1, tiled=True)
+    devices = lax.axis_size("seq")
+    forward = [(i, (i + 1) % devices) for i in range(devices)]
+    blocks = [query_rot]
+    for hop in range(1, devices):
+        blocks = [lax.ppermute(blocks[0], "seq", forward), *blocks]
+    whole = jnp.concatenate(blocks, axis=1)
+    shift = (lax.axis_index("seq") + 1) * blocks[-1].shape[1]
+    query_whole = jnp.roll(whole, shift, axis=1)
     all_rows = query_whole.shape[0] * query_whole.shape[1]
     scores = (
         jnp.einsum(

time: 271 us -> 285 us (1.052)
  waiting for transfers between devices: 42.4 us -> 79.9 us
  blocking collectives: 130 us -> 94 us
  local copies, waits for them, and re-layouts: 28.4 us -> 37.3 us
    all_gather x1 -> x0, blocking collectives: 33.1 us -> none  [body(): query_whole = lax.all_gather(query_rot, 'seq', axis=1, tiled=True)]
    ppermute x0 -> x7, waiting for transfers between devices: none -> 31.8 us  [body(): blocks = [lax.ppermute(blocks[0], 'seq', forward), *blocks]]
    unnamed x30 -> x53, local copies, waits for them, and re-layouts: 5.4 us -> 13.1 us
    unnamed x2, waiting for transfers between devices: 42.4 us -> 48.1 us
    pmax x1, blocking collectives: 36.5 us -> 33.3 us  [body(): top_score = lax.pmax(jnp.max(scores, axis=-1), 'seq')]
  transfers between devices with their start and end apart: 1 -> 8, of which waited for: 1 -> 8; matrix products, arithmetic and copies ran while one was open for 5% -> 10% of each run, Pallas kernels for 0% -> 0%
where the time goes in v1:
time: 285 us; the launch traced here: 284 us
  blocking collectives  94 us (33%)
  waiting for transfers between devices  79.9 us (28%)
  local copies, waits for them, and re-layouts  37.3 us (13%)
  matrix products  33.8 us (12%)
  between operations  18.6 us (7%)
  other arithmetic  18.3 us (6%)
    unnamed x2, waiting for transfers between devices  48.1 us
    unnamed x1, blocking collectives  33.8 us
    pmax x1, blocking collectives, body(): top_score = lax.pmax(jnp.max(scores, axis=-1), 'seq')  33.3 us
    ppermute x7, waiting for transfers between devices, body(): blocks = [lax.ppermute(blocks[0], 'seq', forward), *blocks]  31.8 us
    unnamed x53, local copies, waits for them, and re-layouts  13.1 us
    all_gather x1, blocking collectives, body(): lax.all_gather(hidden_states, 'head', axis=2, tiled=True)  10.7 us
    all_gather x1, blocking collectives, body(): lax.all_gather(clean_states, 'head', axis=2, tiled=True)  9.5 us
    reshape x2, local copies, waits for them, and re-layouts, body(): summed.reshape(group_count, -1, local_inner)  7.71 us
  transfers between devices with their start and end apart: 8, of which 8 were waited for; matrix products, arithmetic and copies ran while one was open for 10% of the time, Pallas kernels for 0%

profile of v1, /device:TPU:0, one launch (start us, length us, event | category | flops | bytes accessed | tf_op | source)
XLA Modules:
  0.0 283.8 jit_solution(8100875769576238494)
XLA Ops:
  7.2 1.9 copy.93
  9.2 1.9 copy.94
  12.5 10.7 %all_gather.6 = bf16[2,44,5120]{2,0,1:T(2,128)(2,1)S(1)} all-gather(bf16[2,44,1280]{2,0,1:T(2,128)(2,1)S(1)} %copy-done.6), channel_id=1, replica_groups=mesh['seq'=8,'head'=4] {'head'}, dimensions={2}, use_global_device_ids=true | all-gather | bytes 1126400 | tf_op jit(solution)/shard_map/all_gather | solution.py:82
  25.7 1.8 fusion.17
  27.8 4.2 %multiply_reduce_fusion.2 = (f32[88]{0:T(128)S(1)}, f32[88,640]{1,0:T(8,128)S(1)}) fusion(bf16[88,5120]{1,0:T(8,128)(2,1)S(1)} %reshape.149, bf16[5120,640]{1,0:T(8,128)(2,1)} %param.15), kind=kOutput, calls=%fused_computation.43 | convolution fusion | flops 576829376 | bytes 7680352 | tf_op jit(solution)/shard_map/dot_general | solution.py:95
  32.0 4.2 %multiply_reduce_fusion.3 = (f32[88]{0:T(128)S(1)}, f32[88,640]{1,0:T(8,128)S(1)}) fusion(bf16[88,5120]{1,0:T(8,128)(2,1)S(1)} %reshape.149, bf16[5120,640]{1,0:T(8,128)(2,1)} %param.14), kind=kOutput, calls=%fused_computation.45 | convolution fusion | flops 576829376 | bytes 7680352 | tf_op jit(solution)/shard_map/dot_general | solution.py:94
  36.2 9.5 %all_gather.7 = bf16[2,44,5120]{2,0,1:T(2,128)(2,1)S(1)} all-gather(bf16[2,44,1280]{2,0,1:T(2,128)(2,1)S(1)} %copy-done.7), channel_id=1, replica_groups=mesh['seq'=8,'head'=4] {'head'}, dimensions={2}, use_global_device_ids=true | all-gather | bytes 1126400 | tf_op jit(solution)/shard_map/all_gather | solution.py:83
  47.8 1.8 fusion.13
  50.0 4.5 %multiply_reduce_fusion.1 = (f32[88]{0:T(128)S(1)}, f32[88,640]{1,0:T(8,128)S(1)}) fusion(bf16[88,5120]{1,0:T(8,128)(2,1)S(1)} %reshape.160, bf16[5120,640]{1,0:T(8,128)(2,1)} %param.15), kind=kOutput, calls=%fused_computation.41 | convolution fusion | flops 576829376 | bytes 7680352 | tf_op jit(solution)/shard_map/dot_general | solution.py:96
  54.5 6.7 %all-reduce.2 = (f32[88]{0:T(128)S(1)}, f32[88]{0:T(128)S(1)}, f32[88]{0:T(128)S(1)}) all-reduce(f32[88]{0:T(128)S(1)} %get-tuple-element.38, f32[88]{0:T(128)S(1)} %get-tuple-element.40, f32[88]{0:T(128)S(1)} %get-tuple-element.42), channel_id=1, replica_groups=mesh['seq'=8,'head'=4] {'head'}, use_global_device_ids=true, to_apply=%region_4.0 | all-reduce | flops 264 | bytes 2112 | tf_op jit(solution)/shard_map/psum | solution.py:99
  65.3 4.7 %convolution_convert_fusion.1 = bf16[88,640]{1,0:T(8,128)(2,1)} fusion(bf16[88,5120]{1,0:T(8,128)(2,1)S(1)} %reshape.149, bf16[5120,640]{1,0:T(8,128)(2,1)} %param.16), kind=kOutput, calls=%fused_computation.27 | convolution fusion | flops 576773120 | bytes 7567360 | tf_op jit(solution)/shard_map/dot_general | solution.py:97
  71.6 1.6 fusion.26
  74.9 4.0 %collective-permute-done.1 = bf16[2,44,640]{2,0,1:T(2,128)(2,1)} collective-permute-done((bf16[2,44,640]{2,0,1:T(2,128)(2,1)S(1)}, bf16[2,44,640]{2,0,1:T(2,128)(2,1)}, u32[]{:S(2)}, u32[]{:S(2)}) %collective-permute-start.1) | collective-permute-done | bytes 112672 | tf_op jit(solution)/shard_map/ppermute | solution.py:151
  78.9 1.7 subtract_convert_fusion
  84.9 1.8 collective-permute-done.2
  87.8 1.7 reshape.151
  89.5 5.3 %collective-permute-done.3 = bf16[2,44,640]{2,0,1:T(2,128)(2,1)S(1)} collective-permute-done((bf16[2,44,640]{2,0,1:T(2,128)(2,1)}, bf16[2,44,640]{2,0,1:T(2,128)(2,1)S(1)}, u32[]{:S(2)}, u32[]{:S(2)}) %collective-permute-start.3) | collective-permute-done | bytes 112672 | tf_op jit(solution)/shard_map/ppermute | solution.py:151
  95.0 8.5 %collective-permute-done.4 = bf16[2,44,640]{2,0,1:T(2,128)(2,1)} collective-permute-done((bf16[2,44,640]{2,0,1:T(2,128)(2,1)S(1)}, bf16[2,44,640]{2,0,1:T(2,128)(2,1)}, u32[]{:S(2)}, u32[]{:S(2)}) %collective-permute-start.4) | collective-permute-done | bytes 112672 | tf_op jit(solution)/shard_map/ppermute | solution.py:151
  104.7 6.6 %collective-permute-done.5 = bf16[2,44,640]{2,0,1:T(2,128)(2,1)S(1)} collective-permute-done((bf16[2,44,640]{2,0,1:T(2,128)(2,1)}, bf16[2,44,640]{2,0,1:T(2,128)(2,1)S(1)}, u32[]{:S(2)}, u32[]{:S(2)}) %collective-permute-start.5) | collective-permute-done | bytes 112672 | tf_op jit(solution)/shard_map/ppermute | solution.py:151
  111.4 1.7 reshape.157
  114.4 4.4 %collective-permute-done.6 = bf16[2,44,640]{2,0,1:T(2,128)(2,1)S(1)} collective-permute-done((bf16[2,44,640]{2,0,1:T(2,128)(2,1)S(1)}, bf16[2,44,640]{2,0,1:T(2,128)(2,1)S(1)}, u32[]{:S(2)}, u32[]{:S(2)}) %collective-permute-start.6) | collective-permute-done | bytes 112672 | tf_op jit(solution)/shard_map/ppermute | solution.py:151
  126.4 1.7 copy.43
  128.9 5.6 %multiply_reduce_fusion = (f32[5,704]{1,0:T(8,128)S(1)}, f32[5,704,484]{2,1,0:T(8,128)}) fusion(bf16[704,5,128]{0,2,1:T(8,128)(2,1)S(1)} %reshape.153, bf16[484,5,128]{2,1,0:T(8,128)(2,1)} %reshape.157), kind=kOutput, calls=%fused_computation.1 | convolution fusion | flops 439545920 | bytes 8349440 | tf_op jit(solution)/shard_map/qhd,khd->hqk/dot_general | solution.py:157
  134.6 33.3 %pmax.7 = f32[5,704]{1,0:T(8,128)S(1)} all-reduce(f32[5,704]{1,0:T(8,128)S(1)} %get-tuple-element.44), channel_id=1, replica_groups=mesh['seq'=8,'head'=4] {'seq'}, use_global_device_ids=true, to_apply=%region_8.0 | all-reduce | flops 3520 | bytes 28160 | tf_op jit(solution)/shard_map/pmax | solution.py:165
  167.9 5.7 %fusion.18 = f32[704,5,128]{2,0,1:T(8,128)} fusion(f32[5,704,484]{2,1,0:T(8,128)} %get-tuple-element.45, f32[5,704]{1,0:T(8,128)S(1)} %pmax.7, bf16[484,5,128]{2,1,0:T(8,128)(2,1)S(1)} %copy-done.1), kind=kOutput, calls=%fused_computation.25 | convolution fusion | flops 441253120 | bytes 9250560 | tf_op jit(solution)/shard_map/hqk,khd->qhd/dot_general | solution.py:168
  173.6 1.9 copy.49
  175.5 2.9 %reshape.158 = f32[2,352,640]{1,0,2:T(2,128)} reshape(f32[704,5,128]{0,2,1:T(8,128)S(1)} %copy.49) | data formatting | bytes 3604480 | tf_op jit(solution)/shard_map/reshape | solution.py:176
  178.4 4.8 %copy.50 = f32[2,352,640]{2,0,1:T(2,128)} copy(f32[2,352,640]{1,0,2:T(2,128)} %reshape.158) | data formatting | bytes 3604480 | tf_op jit(solution)/shard_map/reshape | solution.py:176
  183.3 4.9 %convolution_convert_fusion = bf16[88,640]{1,0:T(8,128)(2,1)S(1)} fusion(bf16[88,5120]{1,0:T(8,128)(2,1)} %copy-done, bf16[5120,640]{1,0:T(8,128)(2,1)} %param.16), kind=kOutput, calls=%fused_computation.26 | convolution fusion | flops 576773120 | bytes 7567360 | tf_op jit(solution)/shard_map/dot_general | solution.py:98
  190.7 2.0 fusion
  192.8 33.8 %all-reduce.1 = f32[2,352,5]{1,0,2:T(2,128)S(1)} all-reduce(f32[2,352,5]{1,0,2:T(2,128)S(1)} %reshape.159), channel_id=3, replica_groups=mesh['seq'=8,'head'=4] {'seq'}, use_global_device_ids=true, to_apply=%region_11.0.clone | all-reduce | flops 3520 | bytes 28160
  227.1 48.1 %all-reduce.5.cloned.1.call-done = f32[2,352,640]{2,0,1:T(2,128)} async-done(((f32[2,352,640]{2,0,1:T(2,128)}), f32[2,352,640]{2,0,1:T(2,128)}) %all-reduce.5.cloned.1.call-update) | async-done | bytes 1802256
  (117 shorter events, 31.4 us)
Async XLA Ops:
  7.2 5.4 %copy-start.6 = (bf16[2,44,1280]{2,0,1:T(2,128)(2,1)S(1)}, bf16[2,44,1280]{2,0,1:T(2,128)(2,1)}, u32[]{:S(2)}) copy-start(bf16[2,44,1280]{2,0,1:T(2,128)(2,1)} %param.12) | copy-start | bytes 675844
  7.2 4.0 %copy-start.9 = (s32[3]{0:T(128)S(1)}, s32[3]{0:T(128)}, u32[]{:S(2)}) copy-start(s32[3]{0:T(128)} %param.22) | copy-start | bytes 40
  7.2 3.9 %copy-start.12 = (s32[11]{0:T(128)S(1)}, s32[11]{0:T(128)}, u32[]{:S(2)}) copy-start(s32[11]{0:T(128)} %param.23) | copy-start | bytes 136
  7.2 268.0 %all-reduce.5.cloned.1.call-start = ((), (), s32[]{:S(2)}) async-start(), calls=%async_computation | async-start | bytes 3604480
  11.1 14.3 %copy-start.8 = (f32[4,2,5120]{2,1,0:T(2,128)S(1)}, f32[4,2,5120]{2,1,0:T(2,128)}, u32[]{:S(2)}) copy-start(f32[4,2,5120]{2,1,0:T(2,128)} %param.21) | copy-start | bytes 491524
  32.0 4.2 %copy-start.7 = (bf16[2,44,1280]{2,0,1:T(2,128)(2,1)S(1)}, bf16[2,44,1280]{2,0,1:T(2,128)(2,1)}, u32[]{:S(2)}) copy-start(bf16[2,44,1280]{2,0,1:T(2,128)(2,1)} %param.13) | copy-start | bytes 675844
  50.0 4.5 %copy-start = (bf16[88,5120]{1,0:T(8,128)(2,1)}, bf16[88,5120]{1,0:T(8,128)(2,1)S(1)}, u32[]{:S(2)}) copy-start(bf16[88,5120]{1,0:T(8,128)(2,1)S(1)} %reshape.160) | copy-start | bytes 2703364
  50.0 11.3 %copy-start.10 = (f32[640]{0:T(1024)S(1)}, f32[640]{0:T(1024)}, u32[]{:S(2)}) copy-start(f32[640]{0:T(1024)} %param.18) | copy-start | bytes 7684
  50.0 12.0 %copy-start.11 = (f32[640]{0:T(1024)S(1)}, f32[640]{0:T(1024)}, u32[]{:S(2)}) copy-start(f32[640]{0:T(1024)} %param.17) | copy-start | bytes 7684
  63.8 7.5 %collective-permute-start = (bf16[2,44,640]{2,0,1:T(2,128)(2,1)S(1)}, bf16[2,44,640]{2,0,1:T(2,128)(2,1)S(1)}, u32[]{:S(2)}, u32[]{:S(2)}) collective-permute-start(bf16[2,44,640]{2,0,1:T(2,128)(2,1)S(1)} %copy.56), channel_id=1, source_target_pairs={{0,4},{4,8},{8,12},{12,16},{16,20},{20,24},{24,28},{28,0},{1,5},{5... | collective-permute-start | bytes 337928 | tf_op jit(solution)/shard_map/ppermute | solution.py:151
  71.3 7.6 %copy-start.4 = (bf16[2,44,640]{2,0,1:T(2,128)(2,1)}, bf16[2,44,640]{2,0,1:T(2,128)(2,1)S(1)}, u32[]{:S(2)}) copy-start(bf16[2,44,640]{2,0,1:T(2,128)(2,1)S(1)} %collective-permute-done) | copy-start | bytes 337924
  71.3 7.6 %collective-permute-start.1 = (bf16[2,44,640]{2,0,1:T(2,128)(2,1)S(1)}, bf16[2,44,640]{2,0,1:T(2,128)(2,1)}, u32[]{:S(2)}, u32[]{:S(2)}) collective-permute-start(bf16[2,44,640]{2,0,1:T(2,128)(2,1)S(1)} %collective-permute-done), channel_id=1, source_target_pairs={{0,4},{4,8},{8,12},{12,16},{16,20},{20,24},{24,28},{28,0},{1,5},{5... | collective-permute-start | bytes 337928 | tf_op jit(solution)/shard_map/ppermute | solution.py:151
  78.9 7.8 %collective-permute-start.2 = (bf16[2,44,640]{2,0,1:T(2,128)(2,1)}, bf16[2,44,640]{2,0,1:T(2,128)(2,1)}, u32[]{:S(2)}, u32[]{:S(2)}) collective-permute-start(bf16[2,44,640]{2,0,1:T(2,128)(2,1)} %collective-permute-done.1), channel_id=1, source_target_pairs={{0,4},{4,8},{8,12},{12,16},{16,20},{20,24},{24,28},{28,0},{1,5},{5... | collective-permute-start | bytes 337928 | tf_op jit(solution)/shard_map/ppermute | solution.py:151
  80.6 14.2 %copy-start.2 = (bf16[2,44,5,64]{3,2,1,0:T(8,128)(2,1)S(1)}, bf16[2,44,5,64]{3,2,1,0:T(8,128)(2,1)}, u32[]{:S(2)}) copy-start(bf16[2,44,5,64]{3,2,1,0:T(8,128)(2,1)} %get-tuple-element.20) | copy-start | bytes 168964
  86.7 8.1 %collective-permute-start.3 = (bf16[2,44,640]{2,0,1:T(2,128)(2,1)}, bf16[2,44,640]{2,0,1:T(2,128)(2,1)S(1)}, u32[]{:S(2)}, u32[]{:S(2)}) collective-permute-start(bf16[2,44,640]{2,0,1:T(2,128)(2,1)} %collective-permute-done.2), channel_id=1, source_target_pairs={{0,4},{4,8},{8,12},{12,16},{16,20},{20,24},{24,28},{28,0},{1,5},{5... | collective-permute-start | bytes 337928 | tf_op jit(solution)/shard_map/ppermute | solution.py:151
  94.8 8.8 %collective-permute-start.4 = (bf16[2,44,640]{2,0,1:T(2,128)(2,1)S(1)}, bf16[2,44,640]{2,0,1:T(2,128)(2,1)}, u32[]{:S(2)}, u32[]{:S(2)}) collective-permute-start(bf16[2,44,640]{2,0,1:T(2,128)(2,1)S(1)} %collective-permute-done.3), channel_id=1, source_target_pairs={{0,4},{4,8},{8,12},{12,16},{16,20},{20,24},{24,28},{28,0},{1,5},{5... | collective-permute-start | bytes 337928 | tf_op jit(solution)/shard_map/ppermute | solution.py:151
  103.5 7.8 %collective-permute-start.5 = (bf16[2,44,640]{2,0,1:T(2,128)(2,1)}, bf16[2,44,640]{2,0,1:T(2,128)(2,1)S(1)}, u32[]{:S(2)}, u32[]{:S(2)}) collective-permute-start(bf16[2,44,640]{2,0,1:T(2,128)(2,1)} %collective-permute-done.4), channel_id=1, source_target_pairs={{0,4},{4,8},{8,12},{12,16},{16,20},{20,24},{24,28},{28,0},{1,5},{5... | collective-permute-start | bytes 337928 | tf_op jit(solution)/shard_map/ppermute | solution.py:151
  104.7 8.4 %copy-start.13 = (u32[32]{0:T(128)S(1)}, u32[32]{0:T(128)}, u32[]{:S(2)}) copy-start(u32[32]{0:T(128)} %constant.77) | copy-start | bytes 388
  111.3 7.5 %collective-permute-start.6 = (bf16[2,44,640]{2,0,1:T(2,128)(2,1)S(1)}, bf16[2,44,640]{2,0,1:T(2,128)(2,1)S(1)}, u32[]{:S(2)}, u32[]{:S(2)}) collective-permute-start(bf16[2,44,640]{2,0,1:T(2,128)(2,1)S(1)} %collective-permute-done.5), channel_id=1, source_target_pairs={{0,4},{4,8},{8,12},{12,16},{16,20},{20,24},{24,28},{28,0},{1,5},{5... | collective-permute-start | bytes 337928 | tf_op jit(solution)/shard_map/ppermute | solution.py:151
  111.4 10.7 %copy-start.5 = (bf16[2,44,640]{2,0,1:T(2,128)(2,1)S(1)}, bf16[2,44,640]{2,0,1:T(2,128)(2,1)}, u32[]{:S(2)}) copy-start(bf16[2,44,640]{2,0,1:T(2,128)(2,1)} %copy-done.4) | copy-start | bytes 337924
  128.9 38.9 %copy-start.1 = (bf16[484,5,128]{2,1,0:T(8,128)(2,1)S(1)}, bf16[484,5,128]{2,1,0:T(8,128)(2,1)}, u32[]{:S(2)}) copy-start(bf16[484,5,128]{2,1,0:T(8,128)(2,1)} %reshape.151) | copy-start | bytes 1858564
  178.4 12.3 %slice-start = ((s8[7208960]{0:T(1024)(128)(4,1)}), s8[3014656]{0:T(1024)(128)(4,1)S(1)}, s32[]{:S(2)}) async-start(s8[7208960]{0:T(1024)(128)(4,1)} %bitcast.50), calls=%async_computation.1 | async-start | bytes 6029312
  183.2 5.6 %copy-start.3 = (bf16[88,640]{1,0:T(8,128)(2,1)S(1)}, bf16[88,640]{1,0:T(8,128)(2,1)}, u32[]{:S(2)}) copy-start(bf16[88,640]{1,0:T(8,128)(2,1)} %get-tuple-element.29) | copy-start | bytes 337924
  183.2 7.5 %slice-start.1 = ((s8[7208960]{0:T(1024)(128)(4,1)}), s8[4194304]{0:T(1024)(128)(4,1)S(1)}, s32[]{:S(2)}) async-start(s8[7208960]{0:T(1024)(128)(4,1)} %bitcast.50), calls=%async_computation.2 | async-start | bytes 8388608
Sparse Core Ops, SparseCore 0:
  183.4 91.7 all-reduce.4
